TPU v7x, 256 devices: a whole 4x4x8 slice. The times are simulated.
256 devices in a mesh: row: 16 (over x_lo, y, core), col: 16 (over x_hi, z).
Axes of the slice: x: 4 (x_hi: 2, x_lo: 2; x = x_hi * 2 + x_lo), y: 4, z: 8, core: 2. Of those that a mesh axis runs over, the one named last changes fastest.
Arguments:
- top_inverse: bfloat16 [16, 16, 16, 16, 128, 128], P('row', None, None, 'col'), as said below
- upper_panel: bfloat16 [3, 16, 16, 128, 128], P(None, 'row', 'col'), may hold values from -0.25 to 0.25
- upper_pattern: int32 [3, 16, 16], P(None, 'row', 'col'), may hold values from 0 to 1
- upper_diagonal: float32 [3, 128, 128], replicated, may hold values from -6 to 6
- lower_panel: bfloat16 [8, 16, 16, 128, 128], P(None, 'row', 'col'), may hold values from -0.25 to 0.25
- lower_pattern: int32 [8, 16, 16], P(None, 'row', 'col'), may hold values from 0 to 1, as said below
- parents: int32 [8], replicated, may hold values from 0 to 2, as said below
- parent_panel: bfloat16 [8, 128, 128], replicated, may hold values from -0.5 to 0.5
- lower_diagonal: float32 [8, 128, 128], replicated, may hold values from -6 to 6
Outputs:
- upper_columns: bfloat16 [3, 16, 16, 128, 128], P(None, 'row', 'col')
- upper_blocks: float32 [3, 128, 128], replicated
- lower_columns: bfloat16 [8, 16, 16, 128, 128], P(None, 'row', 'col')
- lower_cross: float32 [8, 128, 128], replicated
- lower_blocks: float32 [8, 128, 128], replicated
Inputs may be any that keep to these rules, and one draw needn't show every extreme that they name: top_inverse is symmetric: block (I, J) is the transpose of block (J, I). `lower_pattern`: A second-level pattern is zero wherever the pattern of its parent is zero. `parents`: every first-level supernode is the parent of some second-level supernode.
All inputs are finite; a program needn't handle non-finite values.
Results may differ from a plain program's by a relative error of at most 0.0041.
Values may be sent and summed in bfloat16 or wider, within the bound.
A program may use at most 128 MiB of HBM per device.

v0:
```python
import jax
import jax.numpy as jnp
from jax import lax
from jax.sharding import PartitionSpec as P

HIGH = lax.Precision.HIGHEST


def by_rows(top_inverse, panel):
    partial_value = jnp.einsum(
        "aibjxy,kbjyz->iakxz",
        top_inverse,
        lax.all_gather(panel, "row", axis=1, tiled=True),
        preferred_element_type=jnp.float32,
    )
    reduced = lax.psum_scatter(partial_value, "col", scatter_dimension=0, tiled=True)
    return jnp.transpose(reduced, (2, 1, 0, 3, 4))


def upper_part(upper_product, upper_mask, upper_masked, lower_masked, parents):
    upper_columns = (-upper_product * upper_mask).astype(jnp.bfloat16)
    selected = jnp.take(upper_columns, parents, axis=0)
    local_upper = jnp.einsum(
        "ktsxy,ktsxz->kyz", upper_masked, upper_columns, preferred_element_type=jnp.float32
    )
    local_cross = jnp.einsum(
        "mtsxy,mtsxz->myz", selected, lower_masked, preferred_element_type=jnp.float32
    )
    return (upper_columns, selected, local_upper, local_cross)


def lower_part(lower_product, selected, parent_panel, lower_mask, lower_masked):
    extension = jnp.einsum(
        "mtsxy,myz->mtsxz", selected, parent_panel, preferred_element_type=jnp.float32
    )
    lower_columns = (-(lower_product + extension) * lower_mask).astype(jnp.bfloat16)
    local_lower = jnp.einsum(
        "mtsxy,mtsxz->myz", lower_masked, lower_columns, preferred_element_type=jnp.float32
    )
    return (lower_columns, local_lower)


def per_device(
    top_inverse,
    upper_panel,
    upper_pattern,
    upper_diagonal,
    lower_panel,
    lower_pattern,
    parents,
    parent_panel,
    lower_diagonal,
):
    upper_mask = upper_pattern.astype(jnp.float32)[:, :, :, None, None]
    upper_masked = upper_panel * upper_mask.astype(jnp.bfloat16)
    lower_mask = lower_pattern.astype(jnp.float32)[:, :, :, None, None]
    lower_masked = lower_panel * lower_mask.astype(jnp.bfloat16)
    upper_product = by_rows(top_inverse, upper_masked)
    upper_columns, selected, local_upper, local_cross = upper_part(
        upper_product, upper_mask, upper_masked, lower_masked, parents
    )
    summed_upper, summed_cross = lax.psum((local_upper, local_cross), ("row", "col"))
    lower_product = by_rows(top_inverse, lower_masked)
    lower_columns, local_lower = lower_part(
        lower_product, selected, parent_panel, lower_mask, lower_masked
    )
    summed_lower = lax.psum(local_lower, ("row", "col"))
    upper_blocks = upper_diagonal - summed_upper
    panel_wide = parent_panel.astype(jnp.float32)
    parent_blocks = jnp.take(upper_blocks, parents, axis=0)
    lower_cross = -summed_cross - jnp.einsum(
        "mxy,myz->mxz", parent_blocks, panel_wide, precision=HIGH
    )
    lower_blocks = (
        lower_diagonal
        - summed_lower
        - jnp.einsum("myx,myz->mxz", panel_wide, lower_cross, precision=HIGH)
    )
    return (upper_columns, upper_blocks, lower_columns, lower_cross, lower_blocks)


def solution(mesh):
    return jax.shard_map(
        per_device,
        mesh=mesh,
        in_specs=(
            P("row", None, None, "col", None, None),
            P(None, "row", "col", None, None),
            P(None, "row", "col"),
            P(),
            P(None, "row", "col", None, None),
            P(None, "row", "col"),
            P(),
            P(),
            P(),
        ),
        out_specs=(
            P(None, "row", "col", None, None),
            P(),
            P(None, "row", "col", None, None),
            P(),
            P(),
        ),
        check_vma=False,
    )
```

profile of v0, /device:TPU:1, one launch (start us, length us, event | category | flops | bytes accessed | tf_op | source)
XLA Modules:
  0.0 648.7 jit_solution(10669901075646859960)
XLA Ops:
  7.2 0.0 all-gather.3.cloned.1.call-start
  7.2 0.7 fusion.31
  7.9 1.0 copy.49
  8.9 0.7 broadcast_multiply_fusion.1
  9.7 0.0 all-gather.5.cloned.1.call-start
  9.7 1.1 copy.51
  10.9 0.7 convert_bitcast_fusion
  11.5 0.8 broadcast_multiply_fusion
  12.3 0.0 all-reduce.9.cloned.1.call-start
  12.4 37.7 %all-gather.3.cloned.1.call-done = bf16[3,16,1,128,128]{3,4,1,0,2:T(8,128)(2,1)} async-done(((bf16[3,1,1,128,128]{3,4,1,0,2:T(8,128)(2,1)}), bf16[3,16,1,128,128]{3,4,1,0,2:T(8,128)(2,1)}) %all-gather.3.cloned.1.call-update) | async-done | bytes 1572880 | tf_op jit(solution)/shard_map/all_gather | solution.py:13
  50.1 7.5 %fusion.10 = f32[16,1,3,128,128]{3,4,0,2,1:T(8,128)} fusion(bf16[1,16,16,1,128,128]{5,4,3,2,1,0:T(8,128)(2,1)} %param.9, bf16[3,16,1,128,128]{3,4,1,0,2:T(8,128)(2,1)} %all-gather.3.cloned.1.call-done), kind=kOutput, calls=%fused_computation.8 | convolution fusion | flops 3221225472 | bytes 13107200 | tf_op jit(solution)/shard_map/aibjxy,kbjyz->iakxz/dot_general | solution.py:10
  57.5 34.6 %all-gather.5.cloned.1.call-done = bf16[8,16,1,128,128]{3,4,1,0,2:T(8,128)(2,1)} async-done(((bf16[8,1,1,128,128]{3,4,1,0,2:T(8,128)(2,1)}), bf16[8,16,1,128,128]{3,4,1,0,2:T(8,128)(2,1)}) %all-gather.5.cloned.1.call-update) | async-done | bytes 4194320 | tf_op jit(solution)/shard_map/all_gather | solution.py:13
  92.2 13.6 %fusion.5 = f32[16,1,8,128,128]{3,4,0,2,1:T(8,128)} fusion(bf16[1,16,16,1,128,128]{5,4,3,2,1,0:T(8,128)(2,1)} %param.9, bf16[8,16,1,128,128]{3,4,1,0,2:T(8,128)(2,1)} %all-gather.5.cloned.1.call-done), kind=kOutput, calls=%fused_computation.7 | convolution fusion | flops 8589934592 | bytes 20971520 | tf_op jit(solution)/shard_map/aibjxy,kbjyz->iakxz/dot_general | solution.py:10
  105.9 0.0 all-reduce.7.cloned.1.call-start
  105.9 0.6 copy-done.9
  106.5 0.6 dynamic-slice
  107.1 263.9 %all-reduce.9.cloned.1.call-done = (f32[16,1,3,128,128]{3,4,0,2,1:T(8,128)}, f32[16,1,8,128,128]{3,4,0,2,1:T(8,128)}) async-done(((f32[16,1,3,128,128]{3,4,0,2,1:T(8,128)}, f32[16,1,8,128,128]{3,4,0,2,1:T(8,128)}), (f32[16,1,3,128,128]{3,4,0,2,1:T(8,128)}, f32[16,1,8,128,128]{3,4,0,2,1:T(8,128)})) %all-reduce.9.cloned.1.call-update) | async-done | bytes 11534352
  371.0 1.6 constant_dynamic-slice_fusion.1
  372.6 0.1 copy.50
  372.7 0.7 fusion.37
  373.4 0.9 fusion.27
  374.4 1.7 constant_dynamic-slice_fusion
  376.1 0.2 copy.52
  376.3 0.6 gather_fusion
  376.9 1.2 fusion.21
  378.1 0.3 fusion.17
  378.4 1.0 fusion.19
  379.5 257.1 %all-reduce.7.cloned.1.call-done = (f32[3,128,128]{2,1,0:T(8,128)}, f32[8,128,128]{2,1,0:T(8,128)}, f32[8,128,128]{2,1,0:T(8,128)}) async-done(((f32[3,128,128]{2,1,0:T(8,128)}, f32[8,128,128]{2,1,0:T(8,128)}, f32[8,128,128]{2,1,0:T(8,128)}), (f32[3,128,128]{2,1,0:T(8,128)}, f32[8,128,128]{2,1,0:T(8,128)}, f32[8,128,128]{2,1,0:T(8,128)})) %all-reduce.7.cloned.1.call-update) | async-done | bytes 1245200 | tf_op jit(solution)/shard_map/psum | solution.py:62
  636.6 0.9 sub.12
  637.6 0.6 gather_fusion.1
  638.1 1.5 convolution_subtract_fusion
  639.7 2.5 fusion.16
  (26 shorter events, 0.1 us)
Async XLA Ops:
  7.2 371.0 %copy-start = (bf16[8,128,128]{2,1,0:T(8,128)(2,1)S(1)}, bf16[8,128,128]{2,1,0:T(8,128)(2,1)}, u32[]{:S(2)}) copy-start(bf16[8,128,128]{2,1,0:T(8,128)(2,1)} %param.16) | copy-start | bytes 786436
  7.2 42.9 %all-gather.3.cloned.1.call-start = ((), (), s32[]{:S(2)}) async-start(), calls=%async_computation | async-start | bytes 1671168 | tf_op jit(solution)/shard_map/all_gather | solution.py:13
  9.7 82.5 %all-gather.5.cloned.1.call-start = ((), (), s32[]{:S(2)}) async-start(), calls=%async_computation.1 | async-start | bytes 4456448 | tf_op jit(solution)/shard_map/all_gather | solution.py:13
  12.3 358.6 %all-reduce.9.cloned.1.call-start = ((), (), s32[]{:S(2)}) async-start(), calls=%async_computation.3 | async-start | bytes 23068672
  105.8 0.7 copy-start.9
  105.8 1.3 copy-start.8
  105.8 267.6 %copy-start.5 = (bf16[3,1,1,128,128]{3,4,1,0,2:T(8,128)(2,1)S(1)}, bf16[3,1,1,128,128]{3,4,1,0,2:T(8,128)(2,1)}, u32[]{:S(2)}) copy-start(bf16[3,1,1,128,128]{3,4,1,0,2:T(8,128)(2,1)} %broadcast_multiply_fusion.1) | copy-start | bytes 294916
  105.8 271.1 %copy-start.1 = (bf16[8,1,1,128,128]{3,4,1,0,2:T(8,128)(2,1)S(1)}, bf16[8,1,1,128,128]{3,4,1,0,2:T(8,128)(2,1)}, u32[]{:S(2)}) copy-start(bf16[8,1,1,128,128]{3,4,1,0,2:T(8,128)(2,1)} %broadcast_multiply_fusion) | copy-start | bytes 786436
  105.9 530.7 %all-reduce.7.cloned.1.call-start = ((), (), s32[]{:S(2)}) async-start(), calls=%async_computation.2 | async-start | bytes 2490368 | tf_op jit(solution)/shard_map/psum | solution.py:62
  372.6 264.0 %copy-start.7 = (f32[3,128,128]{2,1,0:T(8,128)S(1)}, f32[3,128,128]{2,1,0:T(8,128)}, u32[]{:S(2)}) copy-start(f32[3,128,128]{2,1,0:T(8,128)} %param.12) | copy-start | bytes 589828
  376.9 262.8 %copy-start.6 = (f32[8,128,128]{2,1,0:T(8,128)S(1)}, f32[8,128,128]{2,1,0:T(8,128)}, u32[]{:S(2)}) copy-start(f32[8,128,128]{2,1,0:T(8,128)} %param.17) | copy-start | bytes 1572868
  378.4 263.8 %copy-start.4 = (bf16[8,128,128]{2,1,0:T(8,128)(2,1)}, bf16[8,128,128]{2,1,0:T(8,128)(2,1)S(1)}, u32[]{:S(2)}) copy-start(bf16[8,128,128]{2,1,0:T(8,128)(2,1)S(1)} %fusion.17) | copy-start | bytes 786436
  637.5 4.6 copy-start.2
  639.7 2.5 copy-start.3
Sparse Core Ops, SparseCore 0:
  10.4 39.6 all-gather.2
  52.4 39.6 all-gather.4
  106.0 264.9 all-reduce.8
  379.6 256.9 all-reduce.6
where the time goes:
time: 650 us; the launch traced here: 649 us
  waiting for transfers between devices  593 us (91%)
  matrix products  28.5 us (4%)
  between operations  13.9 us (2%)
  local copies, waits for them, and re-layouts  8.16 us (1%)
    unnamed x5, waiting for transfers between devices  264 us
    psum x1, waiting for transfers between devices, per_device(): lax.psum((local_upper, local_cross), ('row', 'col'))  257 us
    all_gather x2, waiting for transfers between devices, by_rows(): lax.all_gather(panel, 'row', axis=1, tiled=True)  72.3 us
    dot_general x2, matrix products, by_rows(): jnp.einsum('aibjxy,kbjyz->iakxz', top_inverse, lax.all_gather(panel, 'row...  21.1 us
  transfers between devices with their start and end apart: 4, of which 4 were waited for; matrix products, arithmetic and copies ran while one was open for 2% of the time, Pallas kernels for 0%

commit v1 on v0

v1 whole, which is shorter than its diff:
```python
import functools

import jax
import jax.numpy as jnp
from jax import lax
from jax.experimental import pallas as pl
from jax.experimental.pallas import tpu as pltpu
from jax.sharding import PartitionSpec as P

HIGH = lax.Precision.HIGHEST
MESH = pl.DeviceIdType.MESH
F32 = jnp.float32
BF16 = jnp.bfloat16

XL, Y, XH, Z = 2, 4, 2, 8
COLS = XH * Z
PLANE = XH * XL * Y
BLOCK = 128
UPPER, LOWER = 3, 8
PANELS = UPPER + LOWER
UP, DOWN = Z // 2, Z // 2 - 1

CHUNKS = ((0, 1), (1, 2), (3, 2), (5, 2), (7, 2), (9, 2))
STARTS = (0, 1, 3, 5, 7, 9)
SPREAD = (False, False, False, False, False, False)
NC = len(CHUNKS)
FIRST_ROWS = 1536
SECOND_ROWS = LOWER * BLOCK


def kernel(
    top_hbm,
    upper_hbm,
    upper_pattern,
    upper_diagonal_hbm,
    lower_hbm,
    lower_pattern,
    parents,
    parent_panel_hbm,
    lower_diagonal_hbm,
    upper_columns,
    upper_blocks,
    lower_columns,
    lower_cross,
    lower_blocks,
    top,
    panel,
    parent_panel,
    upper_diagonal,
    lower_diagonal,
    masked,
    gathered,
    core_out,
    core_in,
    own_sum,
    y_out,
    y_in,
    x_sum,
    x_in,
    columns_t,
    extension_t,
    base,
    first,
    second,
    load_sem,
    ring_send,
    ring_recv,
    spread_send,
    spread_recv,
    core_send,
    core_recv,
    y_send,
    y_recv,
    x_send,
    x_recv,
    first_sems,
    second_sems,
):
    row = lax.axis_index("row")
    col = lax.axis_index("col")
    co = row % 2
    y = (row // 2) % Y
    xl = row // (2 * Y)
    z = col % Z
    xh = col // Z

    def device(dxl=0, dy=0, dco=0, dxh=0, dz=0):
        r = (((xl + dxl) % XL) * Y + (y + dy) % Y) * 2 + (co + dco) % 2
        c = ((xh + dxh) % XH) * Z + (z + dz) % Z
        return (r, c)

    plane_offsets = [
        (dxh, dxl, dy)
        for dxh in range(XH)
        for dxl in range(XL)
        for dy in range(Y)
        if (dxh, dxl, dy) != (0, 0, 0)
    ]

    loads = []

    def load(src, dst):
        copy = pltpu.make_async_copy(src, dst, load_sem.at[len(loads)])
        copy.start()
        loads.append(copy)

    load(upper_hbm, panel.at[pl.ds(0, UPPER)])
    load(lower_hbm, panel.at[pl.ds(UPPER, LOWER)])
    load(top_hbm.at[:, :, 1 - co], top.at[1])
    load(top_hbm.at[:, :, co], top.at[0])
    load(parent_panel_hbm, parent_panel)
    load(upper_diagonal_hbm, upper_diagonal)
    load(lower_diagonal_hbm, lower_diagonal)

    barrier = pltpu.get_barrier_semaphore()
    partners = [device(dxh=a, dxl=b, dy=c) for a, b, c in plane_offsets]
    partners += [device(dz=d) for d in range(1, Z)] + [device(dco=1)]
    for partner in partners:
        pl.semaphore_signal(barrier, 1, device_id=partner, device_id_type=MESH)

    loads[0].wait()
    loads[1].wait()
    for k in range(PANELS):
        if k < UPPER:
            mask = upper_pattern[k, 0, 0].astype(F32)
        else:
            mask = lower_pattern[k - UPPER, 0, 0].astype(F32)
        wide = panel[k].astype(F32) * mask
        masked[k] = wide.astype(BF16)
        gathered[col, k] = wide.T.astype(BF16)

    pl.semaphore_wait(barrier, len(partners))

    started = []

    def send(src, dst, send_sem, recv_sem, to):
        copy = pltpu.make_async_remote_copy(
            src_ref=src, dst_ref=dst, send_sem=send_sem, recv_sem=recv_sem,
            device_id=to, device_id_type=MESH,
        )
        copy.start()
        started.append(copy)

    def arrive(dst, send_sem, recv_sem):
        pltpu.make_async_remote_copy(
            src_ref=dst, dst_ref=dst, send_sem=send_sem, recv_sem=recv_sem,
            device_id=device(dco=1), device_id_type=MESH,
        ).wait_recv()

    def block(j, plane, dz):
        k0, nk = CHUNKS[j]
        index = ((xh + plane) % XH) * Z + (z + dz) % Z
        return gathered.at[index, pl.ds(k0, nk)]

    def spread_slot(j, dz):
        return spread_send.at[j, dz % Z], spread_recv.at[j, dz % Z]

    def spread(j, dz):
        mine = block(j, 0, dz)
        send(mine, mine, *spread_slot(j, dz), device(dxh=1))

    def ring(j, plane, way, step):
        sign = 1 - 2 * way
        if step:
            arrive(
                block(j, plane, -sign * step),
                ring_send.at[j, plane, way, step - 1],
                ring_recv.at[j, plane, way, step - 1],
            )
            if SPREAD[j]:
                spread(j, -sign * step)
        hops = UP if (way == 0) == (plane == 0) else DOWN
        if step < hops:
            mine = block(j, plane, -sign * step)
            send(
                mine,
                mine,
                ring_send.at[j, plane, way, step],
                ring_recv.at[j, plane, way, step],
                device(dz=sign),
            )

    def ring_event(j, plane, step):
        for way in (0, 1):
            hops = UP if (way == 0) == (plane == 0) else DOWN
            if step <= hops:
                ring(j, plane, way, step)

    def seed(j):
        ring_event(j, 0, 0)
        spread(j, 0)

    def seed_other(j):
        arrive(block(j, 1, 0), *spread_slot(j, 0))
        ring_event(j, 1, 0)

    def collect_spread(j):
        for dz in range(Z):
            arrive(block(j, 1, dz), *spread_slot(j, dz))

    def multiply(j):
        k0, nk = CHUNKS[j]
        ks = pl.ds(k0, nk)

        def product(half, pair):
            left = jnp.concatenate(
                [gathered[i, ks].reshape(nk * BLOCK, BLOCK) for i in range(COLS)], axis=1
            )
            right = jnp.concatenate(
                [top[half, :, 2 * pair + d].reshape(COLS * BLOCK, BLOCK) for d in range(2)],
                axis=1,
            )
            return jnp.dot(left, right, preferred_element_type=F32)

        def theirs(pair, carry):
            out = product(1, pair)
            for d in range(2):
                core_out[2 * pair + d, ks] = (
                    out[:, d * BLOCK : (d + 1) * BLOCK].reshape(nk, BLOCK, BLOCK).astype(BF16)
                )
            return carry

        def ours(pair, carry):
            out = product(0, pair)
            for d in range(2):
                own_sum[2 * pair + d, ks] = out[:, d * BLOCK : (d + 1) * BLOCK].reshape(
                    nk, BLOCK, BLOCK
                )
            return carry

        lax.fori_loop(0, XL * Y // 2, theirs, 0)
        send(
            core_out.at[:, ks], core_in.at[:, ks], core_send.at[j], core_recv.at[j],
            device(dco=1),
        )
        lax.fori_loop(0, XL * Y // 2, ours, 0)

    def add_core(j):
        k0, nk = CHUNKS[j]
        ks = pl.ds(k0, nk)
        arrive(core_in.at[:, ks], core_send.at[j], core_recv.at[j])

        def body(q, carry):
            total = own_sum[q, ks] + core_in[q, ks].astype(F32)
            own_sum[q, ks] = total
            y_out[q // Y, q % Y, ks] = total.astype(BF16)
            return carry

        lax.fori_loop(0, XL * Y, body, 0)
        for dy in (2, 1, 3):
            send(
                y_out.at[:, (y + dy) % Y, ks],
                y_in.at[dy - 1, :, ks],
                y_send.at[j, dy - 1],
                y_recv.at[j, dy - 1],
                device(dy=dy),
            )

    def add_y(j):
        k0, nk = CHUNKS[j]
        ks = pl.ds(k0, nk)
        for dy in range(1, Y):
            arrive(y_in.at[dy - 1, :, ks], y_send.at[j, dy - 1], y_recv.at[j, dy - 1])
        for side in range(XL):
            total = own_sum[side * Y + y, ks]
            for dy in range(1, Y):
                total += y_in[dy - 1, side, ks].astype(F32)
            x_sum[side, ks] = total
        send(
            x_sum.at[1 - xl, ks], x_in.at[ks], x_send.at[j], x_recv.at[j], device(dxl=1)
        )

    def finish(j):
        k0, nk = CHUNKS[j]
        ks = pl.ds(k0, nk)
        arrive(x_in.at[ks], x_send.at[j], x_recv.at[j])
        for k in range(k0, k0 + nk):
            product_t = x_sum[xl, k] + x_in[k]
            if k < UPPER:
                mask = upper_pattern[k, 0, 0].astype(F32)
                wide = -product_t * mask
                columns_t[k] = wide.astype(BF16)
                natural = wide.T.astype(BF16)
                upper_columns[k] = natural
                first[pl.ds(k * BLOCK, BLOCK)] = jnp.dot(
                    gathered[col, k], natural, preferred_element_type=F32
                )
            else:
                m = k - UPPER
                mask = lower_pattern[m, 0, 0].astype(F32)
                natural = (-(product_t + extension_t[m]) * mask).T.astype(BF16)
                lower_columns[m] = natural
                second[pl.ds(m * BLOCK, BLOCK)] = jnp.dot(
                    gathered[col, k], natural, preferred_element_type=F32
                )

    def cross():
        loads[4].wait()
        first[pl.ds(PANELS * BLOCK, FIRST_ROWS - PANELS * BLOCK)] = jnp.zeros(
            (FIRST_ROWS - PANELS * BLOCK, BLOCK), F32
        )
        for m in range(LOWER):
            selected_t = columns_t[parents[m]]
            first[pl.ds((UPPER + m) * BLOCK, BLOCK)] = jnp.dot(
                selected_t, masked[UPPER + m], preferred_element_type=F32
            )
            panel_t = parent_panel[m].astype(F32).T.astype(BF16)
            extension_t[m] = jnp.dot(panel_t, selected_t, preferred_element_type=F32)

    class AllReduce:
        def __init__(self, array, rows, refs):
            self.array, self.rows = array, rows
            self.half, self.piece = rows // 2, rows // 2 // PLANE
            self.core_in, self.half_sum, self.plane_in, self.z_in, self.total = refs[:5]
            self.send, self.recv = refs[5:]
            self.mine = (xh * XL + xl) * Y + y

        def sems(self, i):
            return self.send.at[i], self.recv.at[i]

        def rows_of(self, half, index, count):
            return pl.ds(pl.multiple_of(half * self.half + index * self.piece, 8), count)

        def core(self):
            send(
                self.array.at[self.rows_of(1 - co, 0, self.half)],
                self.core_in,
                *self.sems(0),
                device(dco=1),
            )

        def scatter(self):
            arrive(self.core_in, *self.sems(0))
            self.half_sum[...] = (
                self.array[self.rows_of(co, 0, self.half)] + self.core_in[...]
            )
            for n, (a, b, c) in enumerate(plane_offsets):
                to = (((xh + a) % XH) * XL + (xl + b) % XL) * Y + (y + c) % Y
                send(
                    self.half_sum.at[self.rows_of(0, to, self.piece)],
                    self.plane_in.at[n],
                    *self.sems(1 + n),
                    device(dxh=a, dxl=b, dy=c),
                )

        def exchange(self):
            total = self.half_sum[self.rows_of(0, self.mine, self.piece)]
            for n in range(PLANE - 1):
                arrive(self.plane_in.at[n], *self.sems(1 + n))
                total += self.plane_in[n]
            self.z_in[z] = total
            for dz in range(1, Z):
                send(
                    self.z_in.at[z],
                    self.z_in.at[z],
                    *self.sems(PLANE + dz - 1),
                    device(dz=dz),
                )

        def gather(self):
            for dz in range(1, Z):
                arrive(self.z_in.at[(z - dz) % Z], *self.sems(PLANE + dz - 1))
            total = self.z_in[0]
            for other in range(1, Z):
                total += self.z_in[other]
            place = self.rows_of(co, self.mine, self.piece)
            self.total[place] = total
            for n, (a, b, c) in enumerate(plane_offsets):
                send(
                    self.total.at[place],
                    self.total.at[place],
                    *self.sems(PLANE + Z - 1 + n),
                    device(dxh=a, dxl=b, dy=c),
                )

        def swap(self):
            for n, (a, b, c) in enumerate(plane_offsets):
                source = (((xh - a) % XH) * XL + (xl - b) % XL) * Y + (y - c) % Y
                arrive(
                    self.total.at[self.rows_of(co, source, self.piece)],
                    *self.sems(PLANE + Z - 1 + n),
                )
            ours = self.rows_of(co, 0, self.half)
            send(
                self.total.at[ours], self.total.at[ours], *self.sems(2 * PLANE + Z - 2),
                device(dco=1),
            )

        def end(self):
            arrive(
                self.total.at[self.rows_of(1 - co, 0, self.half)],
                *self.sems(2 * PLANE + Z - 2),
            )

    reduce_first = AllReduce(first, FIRST_ROWS, first_sems)
    reduce_second = AllReduce(second, SECOND_ROWS, second_sems)

    def first_outputs():
        reduce_first.end()
        loads[5].wait()
        loads[6].wait()
        for k in range(UPPER):
            upper_blocks[k] = upper_diagonal[k] - reduce_first.total[pl.ds(k * BLOCK, BLOCK)]
        for m in range(LOWER):
            wide = parent_panel[m].astype(F32)
            value = -reduce_first.total[pl.ds((UPPER + m) * BLOCK, BLOCK)] - jnp.dot(
                upper_blocks[parents[m]], wide, precision=HIGH, preferred_element_type=F32
            )
            lower_cross[m] = value
            base[m] = lower_diagonal[m] - jnp.dot(
                wide.T, value, precision=HIGH, preferred_element_type=F32
            )

    def last_outputs():
        reduce_second.end()
        for m in range(LOWER):
            lower_blocks[m] = base[m] - reduce_second.total[pl.ds(m * BLOCK, BLOCK)]

    events = []

    def at(time, order, what):
        events.append((time, order, len(events), what))

    def wait_top(j):
        if j == 0:
            loads[2].wait()
            loads[3].wait()
        multiply(j)

    for j, start in enumerate(STARTS):
        at(start, 0, functools.partial(seed, j))
        for step in range(1, UP + 1):
            at(start + step, 0, functools.partial(ring_event, j, 0, step))
        if SPREAD[j]:
            ready = start + UP + 1
            at(ready, 0, functools.partial(collect_spread, j))
        else:
            ready = start + 1 + UP
            at(start + 1, 1, functools.partial(seed_other, j))
            for step in range(1, UP + 1):
                at(start + 1 + step, 1, functools.partial(ring_event, j, 1, step))
        at(ready, 4, functools.partial(wait_top, j))
        at(ready + 1, 3, functools.partial(add_core, j))
        at(ready + 2, 2, functools.partial(add_y, j))
        at(ready + 3, 2, functools.partial(finish, j))
    last_upper = max(j for j in range(NC) if CHUNKS[j][0] < UPPER)
    when = STARTS[last_upper] + UP + 1 + 3
    at(when, 2.5, cross)
    at(when, 2.6, reduce_first.core)
    at(when + 1, 2.6, reduce_first.scatter)
    at(when + 2, 2.6, reduce_first.exchange)
    at(when + 3, 2.6, reduce_first.gather)
    at(when + 4, 2.6, reduce_first.swap)
    at(when + 5, 2.6, first_outputs)
    end = max(STARTS[-1] + UP + 1 + 3, when + 5)
    at(end, 5, reduce_second.core)
    at(end + 1, 2.6, reduce_second.scatter)
    at(end + 2, 2.6, reduce_second.exchange)
    at(end + 3, 2.6, reduce_second.gather)
    at(end + 4, 2.6, reduce_second.swap)
    at(end + 5, 2.6, last_outputs)
    for _, _, _, what in sorted(events, key=lambda event: event[:3]):
        what()

    for copy in started:
        copy.wait_send()


def reduce_scratch(rows):
    half = rows // 2
    piece = half // PLANE
    count = 2 * PLANE + Z - 1
    return [
        pltpu.VMEM((half, BLOCK), F32),
        pltpu.VMEM((half, BLOCK), F32),
        pltpu.VMEM((PLANE - 1, piece, BLOCK), F32),
        pltpu.VMEM((Z, piece, BLOCK), F32),
        pltpu.VMEM((rows, BLOCK), F32),
        pltpu.SemaphoreType.DMA((count,)),
        pltpu.SemaphoreType.DMA((count,)),
    ]


def per_device(
    top_inverse,
    upper_panel,
    upper_pattern,
    upper_diagonal,
    lower_panel,
    lower_pattern,
    parents,
    parent_panel,
    lower_diagonal,
):
    square = (BLOCK, BLOCK)
    anywhere = pl.BlockSpec(memory_space=pl.ANY)
    scalars = pl.BlockSpec(memory_space=pltpu.SMEM)
    vector = pl.BlockSpec(memory_space=pltpu.VMEM)
    outs = pl.pallas_call(
        kernel,
        out_shape=(
            jax.ShapeDtypeStruct((UPPER, *square), BF16),
            jax.ShapeDtypeStruct((UPPER, *square), F32),
            jax.ShapeDtypeStruct((LOWER, *square), BF16),
            jax.ShapeDtypeStruct((LOWER, *square), F32),
            jax.ShapeDtypeStruct((LOWER, *square), F32),
        ),
        in_specs=[anywhere, anywhere, scalars, anywhere, anywhere, scalars, scalars, anywhere, anywhere],
        out_specs=(vector,) * 5,
        scratch_shapes=[
            pltpu.VMEM((2, COLS, XL * Y, *square), BF16),
            pltpu.VMEM((PANELS, *square), BF16),
            pltpu.VMEM((LOWER, *square), BF16),
            pltpu.VMEM((UPPER, *square), F32),
            pltpu.VMEM((LOWER, *square), F32),
            pltpu.VMEM((PANELS, *square), BF16),
            pltpu.VMEM((COLS, PANELS, *square), BF16),
            pltpu.VMEM((XL * Y, PANELS, *square), BF16),
            pltpu.VMEM((XL * Y, PANELS, *square), BF16),
            pltpu.VMEM((XL * Y, PANELS, *square), F32),
            pltpu.VMEM((XL, Y, PANELS, *square), BF16),
            pltpu.VMEM((Y - 1, XL, PANELS, *square), BF16),
            pltpu.VMEM((XL, PANELS, *square), F32),
            pltpu.VMEM((PANELS, *square), F32),
            pltpu.VMEM((UPPER, *square), BF16),
            pltpu.VMEM((LOWER, *square), F32),
            pltpu.VMEM((LOWER, *square), F32),
            pltpu.VMEM((FIRST_ROWS, BLOCK), F32),
            pltpu.VMEM((SECOND_ROWS, BLOCK), F32),
            pltpu.SemaphoreType.DMA((7,)),
            pltpu.SemaphoreType.DMA((NC, 2, 2, UP)),
            pltpu.SemaphoreType.DMA((NC, 2, 2, UP)),
            pltpu.SemaphoreType.DMA((NC, Z)),
            pltpu.SemaphoreType.DMA((NC, Z)),
            pltpu.SemaphoreType.DMA((NC,)),
            pltpu.SemaphoreType.DMA((NC,)),
            pltpu.SemaphoreType.DMA((NC, Y - 1)),
            pltpu.SemaphoreType.DMA((NC, Y - 1)),
            pltpu.SemaphoreType.DMA((NC,)),
            pltpu.SemaphoreType.DMA((NC,)),
            reduce_scratch(FIRST_ROWS),
            reduce_scratch(SECOND_ROWS),
        ],
        compiler_params=pltpu.CompilerParams(
            collective_id=0, has_side_effects=True, vmem_limit_bytes=62 * 1024 * 1024
        ),
        name="sweep",
    )(
        top_inverse.reshape(COLS, XL * Y, 2, *square),
        upper_panel.reshape(UPPER, *square),
        upper_pattern,
        upper_diagonal,
        lower_panel.reshape(LOWER, *square),
        lower_pattern,
        parents,
        parent_panel,
        lower_diagonal,
    )
    return (
        outs[0].reshape(UPPER, 1, 1, *square),
        outs[1],
        outs[2].reshape(LOWER, 1, 1, *square),
        outs[3],
        outs[4],
    )


def solution(mesh):
    return jax.shard_map(
        per_device,
        mesh=mesh,
        in_specs=(
            P("row", None, None, "col", None, None),
            P(None, "row", "col", None, None),
            P(None, "row", "col"),
            P(),
            P(None, "row", "col", None, None),
            P(None, "row", "col"),
            P(),
            P(),
            P(),
        ),
        out_specs=(
            P(None, "row", "col", None, None),
            P(),
            P(None, "row", "col", None, None),
            P(),
            P(),
        ),
        check_vma=False,
    )
```

time: 650 us -> 157 us (0.24)
  waiting for transfers between devices: 593 us -> 0 us
  Pallas kernels: 0 us -> 145 us
  matrix products: 28.5 us -> 0 us
  between operations: 13.9 us -> 0.64 us
    unnamed x5 -> x0, waiting for transfers between devices: 264 us -> none
    psum x1 -> x0, waiting for transfers between devices: 257 us -> none  [per_device(): lax.psum((local_upper, local_cross), ('row', 'col'))]
    pallas_call x0 -> x1, Pallas kernels: none -> 145 us  [per_device(): pl.pallas_call(kernel, out_shape=(jax.ShapeDtypeStruct((UPPER, *square),...]
    all_gather x2 -> x0, waiting for transfers between devices: 72.3 us -> none  [by_rows(): lax.all_gather(panel, 'row', axis=1, tiled=True)]
    dot_general x8 -> x0, matrix products: 28.5 us -> none  [the longest x2 21.1 us: by_rows(): jnp.einsum('aibjxy,kbjyz->iakxz', top_inverse, lax.all_gather(panel, 'row...]
  transfers between devices with their start and end apart: 4 -> 0, of which waited for: 4 -> 0; matrix products, arithmetic and copies ran while one was open for 2% -> 0% of each run, Pallas kernels for 0% -> 0%
where the time goes in v1:
time: 157 us
  Pallas kernels  145 us (92%)
  local copies, waits for them, and re-layouts  11.2 us (7%)
    pallas_call x1, Pallas kernels, per_device(): pl.pallas_call(kernel, out_shape=(jax.ShapeDtypeStruct((UPPER, *square),...  145 us
    unnamed x7, local copies, waits for them, and re-layouts  11.2 us

profile of v1, /device:TPU:1, one launch (start us, length us, event | category | flops | bytes accessed | tf_op | source)
XLA Modules:
  0.0 157.2 jit_solution(10811075525353767536)
XLA Ops:
  0.6 1.3 copy.14.upper_pattern
  1.9 1.3 copy.15.lower_pattern
  3.2 145.3 %sweep.1 = (bf16[3,128,128]{2,1,0:T(8,128)(2,1)}, f32[3,128,128]{2,1,0:T(8,128)}, bf16[8,128,128]{2,1,0:T(8,128)(2,1)}, f32[8,128,128]{2,1,0:T(8,128)}, f32[8,128,128]{2,1,0:T(8,128)}) custom-call(bf16[16,8,2,128,128]{4,3,2,1,0:T(8,128)(2,1)} %bitcast.9, bf16[3,128,128]{2,1,0:T(8,128)(2,1)} %bitcast.12, s32[3,1,1]{2,1,0:T(1,128)} %copy.14.upper_pattern, ...), custom_call_target="tpu_custom_call" | custom-call | tf_op jit(solution)/shard_map/sweep/pallas_call | solution.py:499
  148.6 1.5 copy.23
  150.1 1.6 %copy.24 = f32[3,128,128]{2,1,0:T(8,128)} copy(f32[3,128,128]{2,1,0:T(8,128)} %get-tuple-element.26) | data formatting | bytes 393216
  151.8 1.7 %copy.25 = bf16[8,1,1,128,128]{4,3,2,1,0:T(8,128)(2,1)} copy(bf16[8,1,1,128,128]{4,3,2,1,0:T(8,128)(2,1)} %bitcast.11) | data formatting | bytes 524288
  153.4 1.9 %copy.26 = f32[8,128,128]{2,1,0:T(8,128)} copy(f32[8,128,128]{2,1,0:T(8,128)} %get-tuple-element.28) | data formatting | bytes 1048576
  155.3 1.9 %copy.27 = f32[8,128,128]{2,1,0:T(8,128)} copy(f32[8,128,128]{2,1,0:T(8,128)} %get-tuple-element.29) | data formatting | bytes 1048576

commit v2 on v1

v2 whole, which is shorter than its diff:
```python
import functools

import jax
import jax.numpy as jnp
from jax import lax
from jax.experimental import pallas as pl
from jax.experimental.pallas import tpu as pltpu
from jax.sharding import PartitionSpec as P

HIGH = lax.Precision.HIGHEST
MESH = pl.DeviceIdType.MESH
F32 = jnp.float32
BF16 = jnp.bfloat16

XL, Y, XH, Z = 2, 4, 2, 8
COLS = XH * Z
PLANE = XH * XL * Y
BLOCK = 128
UPPER, LOWER = 3, 8
PANELS = UPPER + LOWER
UP, DOWN = Z // 2, Z // 2 - 1

CHUNKS = ((0, 1), (1, 2), (3, 2), (5, 2), (7, 2), (9, 1), (10, 1))
SPREAD = (True, False, True, True, False, True, False)
NC = len(CHUNKS)
LATE = 4
ORDER = (
    ("seed", 0), ("seed", 1), ("seed", 2), ("ring", 0, 0, 1), ("ring", 1, 0, 1),
    ("seed_other", 1), ("ring", 2, 0, 1), ("ring", 0, 0, 2), ("ring", 1, 0, 2),
    ("ring", 1, 1, 1), ("ring", 2, 0, 2), ("ring", 0, 0, 3), ("ring", 1, 0, 3),
    ("ring", 1, 1, 2), ("ring", 2, 0, 3), ("ring", 0, 0, 4), ("ring", 1, 0, 4), ("seed", 3),
    ("ring", 1, 1, 3), ("ring", 2, 0, 4), ("seed", 4), ("m0", 0), ("ring", 3, 0, 1), ("m1", 0),
    ("ring", 1, 1, 4), ("m0", 1), ("ring", 3, 0, 2), ("ring", 4, 0, 1), ("seed_other", 4),
    ("e", 0), ("m1", 1), ("m0", 2), ("ring", 3, 0, 3), ("e", 1), ("m1", 2), ("ring", 4, 0, 2),
    ("ring", 4, 1, 1), ("f", 0), ("e", 2), ("ring", 3, 0, 4), ("seed", 5), ("ring", 4, 0, 3),
    ("h", 0), ("ring", 4, 1, 2), ("ring", 5, 0, 1), ("m0", 3), ("ring", 4, 0, 4), ("seed", 6),
    ("f", 1), ("ring", 4, 1, 3), ("m1", 3), ("ring", 5, 0, 2), ("ring", 6, 0, 1), ("e", 3),
    ("seed_other", 6), ("ring", 4, 1, 4), ("m0", 4), ("ring", 5, 0, 3), ("ring", 6, 0, 2),
    ("h", 1), ("ring", 6, 1, 1), ("cross",), ("f", 2), ("a", 0), ("m1", 4), ("ring", 5, 0, 4),
    ("ring", 6, 0, 3), ("e", 4), ("ring", 6, 1, 2), ("a", 1), ("ring", 6, 0, 4), ("f", 3),
    ("h", 2), ("ring", 6, 1, 3), ("m0", 5), ("ring", 6, 1, 4), ("m1", 5), ("m0", 6), ("e", 5),
    ("m1", 6), ("f", 4), ("e", 6), ("h", 3), ("b", 0), ("h", 4), ("a", 2), ("f", 5), ("f", 6),
    ("h", 5), ("h", 6), ("c", 0), ("a", 3), ("b", 1), ("b", 2), ("c", 1), ("a", 4), ("c", 2),
    ("a", 5), ("b", 3), ("c", 3),
)
FIRST_ROWS = 1536
SECOND_ROWS = (LOWER - LATE) * BLOCK
THIRD_ROWS = LATE * BLOCK
GROUP = 2 * PLANE


def kernel(
    top_hbm,
    upper_hbm,
    upper_pattern,
    upper_diagonal_hbm,
    lower_hbm,
    lower_pattern,
    parents,
    parent_panel_hbm,
    lower_diagonal_hbm,
    upper_columns_hbm,
    upper_blocks_hbm,
    lower_columns_hbm,
    lower_cross_hbm,
    lower_blocks_hbm,
    upper_columns,
    upper_blocks,
    lower_columns,
    lower_cross,
    lower_blocks,
    store_sem,
    top,
    panel,
    parent_panel,
    upper_diagonal,
    lower_diagonal,
    masked,
    gathered,
    core_out,
    core_in,
    own_sum,
    y_out,
    y_in,
    x_sum,
    x_in,
    columns_t,
    extension_t,
    base,
    first,
    second,
    third,
    load_sem,
    ring_send,
    ring_recv,
    spread_recv,
    core_send,
    core_recv,
    y_send,
    y_recv,
    x_send,
    x_recv,
    first_sems,
    second_sems,
    third_sems,
):
    row = lax.axis_index("row")
    col = lax.axis_index("col")
    co = row % 2
    y = (row // 2) % Y
    xl = row // (2 * Y)
    z = col % Z
    xh = col // Z

    def device(dxl=0, dy=0, dco=0, dxh=0, dz=0):
        r = (((xl + dxl) % XL) * Y + (y + dy) % Y) * 2 + (co + dco) % 2
        c = ((xh + dxh) % XH) * Z + (z + dz) % Z
        return (r, c)

    plane_offsets = [
        (dxh, dxl, dy)
        for dxh in range(XH)
        for dxl in range(XL)
        for dy in range(Y)
        if (dxh, dxl, dy) != (0, 0, 0)
    ]

    loads = []

    def load(src, dst):
        copy = pltpu.make_async_copy(src, dst, load_sem.at[len(loads)])
        copy.start()
        loads.append(copy)

    load(upper_hbm, panel.at[pl.ds(0, UPPER)])
    load(lower_hbm, panel.at[pl.ds(UPPER, LOWER)])
    load(top_hbm.at[:, :, 1 - co], top.at[1])
    load(top_hbm.at[:, :, co], top.at[0])
    load(parent_panel_hbm, parent_panel)
    load(upper_diagonal_hbm, upper_diagonal)
    load(lower_diagonal_hbm, lower_diagonal)

    stores = []

    def store(src, dst):
        copy = pltpu.make_async_copy(src, dst, store_sem.at[len(stores)])
        copy.start()
        stores.append(copy)

    barrier = pltpu.get_barrier_semaphore()
    partners = [device(dxh=a, dxl=b, dy=c) for a, b, c in plane_offsets]
    partners += [device(dz=d) for d in range(1, Z)] + [device(dco=1)]
    for partner in partners:
        pl.semaphore_signal(barrier, 1, device_id=partner, device_id_type=MESH)

    loads[0].wait()
    loads[1].wait()
    for k in range(PANELS):
        if k < UPPER:
            mask = upper_pattern[k].astype(F32)
        else:
            mask = lower_pattern[k - UPPER].astype(F32)
        wide = panel[k].astype(F32) * mask
        masked[k] = wide.astype(BF16)
        gathered[col, k] = wide.T.astype(BF16)

    pl.semaphore_wait(barrier, len(partners))

    sent = []

    def send(src, dst, send_sem, recv_sem, to):
        pltpu.make_async_remote_copy(
            src_ref=src, dst_ref=dst, send_sem=send_sem, recv_sem=recv_sem,
            device_id=to, device_id_type=MESH,
        ).start()

    def leave(extent, send_sem):
        sent.append((extent, send_sem))

    def arrive(extent, recv_sem):
        pltpu.make_async_remote_copy(
            src_ref=extent, dst_ref=extent, send_sem=recv_sem, recv_sem=recv_sem,
            device_id=device(dco=1), device_id_type=MESH,
        ).wait_recv()

    def block(j, plane, dz):
        k0, nk = CHUNKS[j]
        index = ((xh + plane) % XH) * Z + (z + dz) % Z
        return gathered.at[index, pl.ds(k0, nk)]

    def blocks(j, count):
        k0, nk = CHUNKS[j]
        return gathered.at[pl.ds(0, count), pl.ds(k0, nk)]

    def spread(j, dz):
        mine = block(j, 0, dz)
        send(mine, mine, ring_send.at[j], spread_recv.at[j], device(dxh=1))

    def ring_event(j, plane, step):
        hops = {1: UP, -1: DOWN} if plane == 0 else {1: DOWN, -1: UP}
        if step:
            ways = [way for way in hops if step <= hops[way]]
            arrive(blocks(j, len(ways)), ring_recv.at[j, plane, step - 1])
            if SPREAD[j]:
                for way in ways:
                    spread(j, -way * step)
        for way in hops:
            if step < hops[way]:
                mine = block(j, plane, -way * step)
                send(mine, mine, ring_send.at[j], ring_recv.at[j, plane, step], device(dz=way))

    def seed(j):
        ring_event(j, 0, 0)
        spread(j, 0)
        leave(blocks(j, COLS - 1), ring_send.at[j])

    def seed_other(j):
        arrive(blocks(j, 1), spread_recv.at[j])
        ring_event(j, 1, 0)

    def collect_spread(j):
        arrive(blocks(j, Z), spread_recv.at[j])

    def multiply(j, part):
        k0, nk = CHUNKS[j]
        ks = pl.ds(k0, nk)

        def product(half, pair):
            left = jnp.concatenate(
                [gathered[i, ks].reshape(nk * BLOCK, BLOCK) for i in range(COLS)], axis=1
            )
            right = jnp.concatenate(
                [top[half, :, 2 * pair + d].reshape(COLS * BLOCK, BLOCK) for d in range(2)],
                axis=1,
            )
            return jnp.dot(left, right, preferred_element_type=F32)

        def theirs(pair, carry):
            out = product(1, pair)
            for d in range(2):
                core_out[2 * pair + d, ks] = (
                    out[:, d * BLOCK : (d + 1) * BLOCK].reshape(nk, BLOCK, BLOCK).astype(BF16)
                )
            return carry

        def ours(pair, carry):
            out = product(0, pair)
            for d in range(2):
                own_sum[2 * pair + d, ks] = out[:, d * BLOCK : (d + 1) * BLOCK].reshape(
                    nk, BLOCK, BLOCK
                )
            return carry

        if part == 0:
            lax.fori_loop(0, XL * Y // 2, theirs, 0)
            send(
                core_out.at[:, ks], core_in.at[:, ks], core_send.at[0], core_recv.at[j],
                device(dco=1),
            )
        else:
            lax.fori_loop(0, XL * Y // 2, ours, 0)

    def add_core(j):
        k0, nk = CHUNKS[j]
        ks = pl.ds(k0, nk)
        arrive(core_in.at[:, ks], core_recv.at[j])

        def body(q, carry):
            total = own_sum[q, ks] + core_in[q, ks].astype(F32)
            own_sum[q, ks] = total
            y_out[q // Y, q % Y, ks] = total.astype(BF16)
            return carry

        lax.fori_loop(0, XL * Y, body, 0)
        for dy in (2, 1, 3):
            send(
                y_out.at[:, (y + dy) % Y, ks],
                y_in.at[dy - 1, :, ks],
                y_send.at[0],
                y_recv.at[j],
                device(dy=dy),
            )

    def add_y(j):
        k0, nk = CHUNKS[j]
        ks = pl.ds(k0, nk)
        arrive(y_in.at[:, :, ks], y_recv.at[j])
        for side in range(XL):
            total = own_sum[side * Y + y, ks]
            for dy in range(1, Y):
                total += y_in[dy - 1, side, ks].astype(F32)
            x_sum[side, ks] = total
        send(
            x_sum.at[1 - xl, ks], x_in.at[ks], x_send.at[0], x_recv.at[j], device(dxl=1)
        )

    def finish(j):
        k0, nk = CHUNKS[j]
        ks = pl.ds(k0, nk)
        arrive(x_in.at[ks], x_recv.at[j])
        for k in range(k0, k0 + nk):
            product_t = x_sum[xl, k] + x_in[k]
            if k < UPPER:
                mask = upper_pattern[k].astype(F32)
                wide = -product_t * mask
                columns_t[k] = wide.astype(BF16)
                natural = wide.T.astype(BF16)
                upper_columns[k] = natural
                first[pl.ds(k * BLOCK, BLOCK)] = jnp.dot(
                    gathered[col, k], natural, preferred_element_type=F32
                )
            else:
                m = k - UPPER
                mask = lower_pattern[m].astype(F32)
                natural = (-(product_t + extension_t[m]) * mask).T.astype(BF16)
                lower_columns[m] = natural
                sums, at_row = (second, m) if m < LOWER - LATE else (third, m - LOWER + LATE)
                sums[pl.ds(at_row * BLOCK, BLOCK)] = jnp.dot(
                    gathered[col, k], natural, preferred_element_type=F32
                )
        if k0 < UPPER:
            store(upper_columns.at[ks], upper_columns_hbm.at[ks])
        else:
            ms = pl.ds(k0 - UPPER, nk)
            store(lower_columns.at[ms], lower_columns_hbm.at[ms])

    def cross():
        loads[4].wait()
        first[pl.ds(PANELS * BLOCK, FIRST_ROWS - PANELS * BLOCK)] = jnp.zeros(
            (FIRST_ROWS - PANELS * BLOCK, BLOCK), F32
        )
        for m in range(LOWER):
            selected_t = columns_t[parents[m]]
            first[pl.ds((UPPER + m) * BLOCK, BLOCK)] = jnp.dot(
                selected_t, masked[UPPER + m], preferred_element_type=F32
            )
            panel_t = parent_panel[m].astype(F32).T.astype(BF16)
            extension_t[m] = jnp.dot(panel_t, selected_t, preferred_element_type=F32)

    class AllReduce:
        def __init__(self, array, rows, refs):
            self.array, self.rows = array, rows
            self.half, self.piece = rows // 2, rows // 2 // PLANE
            self.core_in, self.half_sum, self.plane_in, self.z_in, self.total = refs[:5]
            self.send, self.recv = refs[5:]
            self.mine = (xh * XL + xl) * Y + y

        def sems(self, i):
            return self.send.at[i], self.recv.at[i]

        def rows_of(self, half, index, count):
            return pl.ds(pl.multiple_of(half * self.half + index * self.piece, 8), count)

        def core(self):
            send(
                self.array.at[self.rows_of(1 - co, 0, self.half)],
                self.core_in,
                *self.sems(0),
                device(dco=1),
            )
            leave(self.core_in, self.send.at[0])

        def scatter(self):
            arrive(self.core_in, self.recv.at[0])
            self.half_sum[...] = (
                self.array[self.rows_of(co, 0, self.half)] + self.core_in[...]
            )
            for n, (a, b, c) in enumerate(plane_offsets):
                to = (((xh + a) % XH) * XL + (xl + b) % XL) * Y + (y + c) % Y
                send(
                    self.half_sum.at[self.rows_of(0, to, self.piece)],
                    self.plane_in.at[n],
                    *self.sems(1),
                    device(dxh=a, dxl=b, dy=c),
                )
            leave(self.plane_in, self.send.at[1])

        def exchange(self):
            arrive(self.plane_in, self.recv.at[1])
            total = self.half_sum[self.rows_of(0, self.mine, self.piece)]
            for n in range(PLANE - 1):
                total += self.plane_in[n]
            self.z_in[z] = total
            for dz in (4, 3, 5, 2, 6, 1, 7):
                send(self.z_in.at[z], self.z_in.at[z], *self.sems(2), device(dz=dz))
            leave(self.z_in.at[pl.ds(0, Z - 1)], self.send.at[2])

        def gather(self):
            arrive(self.z_in.at[pl.ds(0, Z - 1)], self.recv.at[2])
            total = self.z_in[0]
            for other in range(1, Z):
                total += self.z_in[other]
            place = self.rows_of(co, self.mine, self.piece)
            self.total[place] = total
            for a, b, c in plane_offsets:
                send(
                    self.total.at[place],
                    self.total.at[place],
                    *self.sems(3),
                    device(dxh=a, dxl=b, dy=c),
                )
            leave(self.plane_in, self.send.at[3])

        def swap(self):
            arrive(self.plane_in, self.recv.at[3])
            ours = self.rows_of(co, 0, self.half)
            send(self.total.at[ours], self.total.at[ours], *self.sems(4), device(dco=1))
            leave(self.core_in, self.send.at[4])

        def end(self):
            arrive(self.core_in, self.recv.at[4])

    group_offsets = [(0, 0, 0, 1)] + [
        (*offset, d) for offset in plane_offsets for d in range(2)
    ]

    class ShortAllReduce:
        def __init__(self, array, rows, refs):
            self.array, self.piece = array, rows // GROUP
            self.group_in, self.z_in, self.total, self.send, self.recv = refs

        def sems(self, i):
            return self.send.at[i], self.recv.at[i]

        def place(self, a, b, c, d):
            index = ((((xh + a) % XH) * XL + (xl + b) % XL) * Y + (y + c) % Y) * 2
            index = index + (co + d) % 2
            return pl.ds(pl.multiple_of(index * self.piece, 8), self.piece)

        def scatter(self):
            for n, (a, b, c, d) in enumerate(group_offsets):
                send(
                    self.array.at[self.place(a, b, c, d)],
                    self.group_in.at[n],
                    *self.sems(0),
                    device(dxh=a, dxl=b, dy=c, dco=d),
                )
            leave(self.group_in, self.send.at[0])

        def exchange(self):
            arrive(self.group_in, self.recv.at[0])
            total = self.array[self.place(0, 0, 0, 0)]
            for n in range(GROUP - 1):
                total += self.group_in[n]
            self.z_in[z] = total
            for dz in (4, 3, 5, 2, 6, 1, 7):
                send(self.z_in.at[z], self.z_in.at[z], *self.sems(1), device(dz=dz))
            leave(self.z_in.at[pl.ds(0, Z - 1)], self.send.at[1])

        def gather(self):
            arrive(self.z_in.at[pl.ds(0, Z - 1)], self.recv.at[1])
            total = self.z_in[0]
            for other in range(1, Z):
                total += self.z_in[other]
            place = self.place(0, 0, 0, 0)
            self.total[place] = total
            for a, b, c, d in group_offsets:
                send(
                    self.total.at[place],
                    self.total.at[place],
                    *self.sems(2),
                    device(dxh=a, dxl=b, dy=c, dco=d),
                )
            leave(self.group_in, self.send.at[2])

        def end(self):
            arrive(self.group_in, self.recv.at[2])

    reduce_third = ShortAllReduce(third, THIRD_ROWS, third_sems)
    reduce_first = AllReduce(first, FIRST_ROWS, first_sems)
    reduce_second = ShortAllReduce(second, SECOND_ROWS, second_sems)

    def first_outputs():
        reduce_first.end()
        loads[5].wait()
        loads[6].wait()
        for k in range(UPPER):
            upper_blocks[k] = upper_diagonal[k] - reduce_first.total[pl.ds(k * BLOCK, BLOCK)]
        for m in range(LOWER):
            wide = parent_panel[m].astype(F32)
            value = -reduce_first.total[pl.ds((UPPER + m) * BLOCK, BLOCK)] - jnp.dot(
                upper_blocks[parents[m]], wide, precision=HIGH, preferred_element_type=F32
            )
            lower_cross[m] = value
            base[m] = lower_diagonal[m] - jnp.dot(
                wide.T, value, precision=HIGH, preferred_element_type=F32
            )
        store(upper_blocks, upper_blocks_hbm)
        store(lower_cross, lower_cross_hbm)

    def outputs(reduction, m0, count):
        reduction.end()
        for m in range(count):
            lower_blocks[m0 + m] = base[m0 + m] - reduction.total[pl.ds(m * BLOCK, BLOCK)]
        ms = pl.ds(m0, count)
        store(lower_blocks.at[ms], lower_blocks_hbm.at[ms])

    def first_multiply(j):
        if SPREAD[j]:
            collect_spread(j)
        if j == min(step[1] for step in ORDER if step[0] == "m0"):
            loads[2].wait()
            loads[3].wait()
        multiply(j, 0)

    first_stages = (reduce_first.core, reduce_first.scatter, reduce_first.exchange,
                    reduce_first.gather, reduce_first.swap, first_outputs)

    def short_stages(reduction, m0, count):
        return (reduction.scatter, reduction.exchange, reduction.gather,
                functools.partial(outputs, reduction, m0, count))

    second_stages = short_stages(reduce_second, 0, LOWER - LATE)
    third_stages = short_stages(reduce_third, LOWER - LATE, LATE)
    work = {
        "seed": seed,
        "ring": ring_event,
        "seed_other": seed_other,
        "m0": first_multiply,
        "m1": lambda j: multiply(j, 1),
        "e": add_core,
        "f": add_y,
        "h": finish,
        "cross": cross,
        "a": lambda i: first_stages[i](),
        "b": lambda i: second_stages[i](),
        "c": lambda i: third_stages[i](),
    }
    for what, *args in ORDER:
        work[what](*args)

    leave(core_out, core_send.at[0])
    leave(y_in, y_send.at[0])
    leave(x_in, x_send.at[0])
    for extent, send_sem in sent:
        pltpu.make_async_remote_copy(
            src_ref=extent, dst_ref=extent, send_sem=send_sem, recv_sem=send_sem,
            device_id=device(dco=1), device_id_type=MESH,
        ).wait_send()
    for copy in stores:
        copy.wait()


def reduce_scratch(rows):
    half = rows // 2
    piece = half // PLANE
    count = 5
    return [
        pltpu.VMEM((half, BLOCK), F32),
        pltpu.VMEM((half, BLOCK), F32),
        pltpu.VMEM((PLANE - 1, piece, BLOCK), F32),
        pltpu.VMEM((Z, piece, BLOCK), F32),
        pltpu.VMEM((rows, BLOCK), F32),
        pltpu.SemaphoreType.DMA((count,)),
        pltpu.SemaphoreType.DMA((count,)),
    ]


def short_reduce_scratch(rows):
    piece = rows // GROUP
    count = 3
    return [
        pltpu.VMEM((GROUP - 1, piece, BLOCK), F32),
        pltpu.VMEM((Z, piece, BLOCK), F32),
        pltpu.VMEM((rows, BLOCK), F32),
        pltpu.SemaphoreType.DMA((count,)),
        pltpu.SemaphoreType.DMA((count,)),
    ]


def finalize(*refs):
    count = len(refs) // 2
    for source, target in zip(refs[:count], refs[count:]):
        target[...] = source[...]


def per_device(
    top_inverse,
    upper_panel,
    upper_pattern,
    upper_diagonal,
    lower_panel,
    lower_pattern,
    parents,
    parent_panel,
    lower_diagonal,
):
    square = (BLOCK, BLOCK)
    anywhere = pl.BlockSpec(memory_space=pl.ANY)
    scalars = pl.BlockSpec(memory_space=pltpu.SMEM)
    vector = pl.BlockSpec(memory_space=pltpu.VMEM)
    out_shape = (
        jax.ShapeDtypeStruct((UPPER, *square), BF16),
        jax.ShapeDtypeStruct((UPPER, *square), F32),
        jax.ShapeDtypeStruct((LOWER, *square), BF16),
        jax.ShapeDtypeStruct((LOWER, *square), F32),
        jax.ShapeDtypeStruct((LOWER, *square), F32),
    )
    outs = pl.pallas_call(
        kernel,
        out_shape=out_shape,
        in_specs=[anywhere, anywhere, scalars, anywhere, anywhere, scalars, scalars, anywhere, anywhere],
        out_specs=(anywhere,) * 5,
        scratch_shapes=[
            *(pltpu.VMEM(array.shape, array.dtype) for array in out_shape),
            pltpu.SemaphoreType.DMA((NC + 4,)),
            pltpu.VMEM((2, COLS, XL * Y, *square), BF16),
            pltpu.VMEM((PANELS, *square), BF16),
            pltpu.VMEM((LOWER, *square), BF16),
            pltpu.VMEM((UPPER, *square), F32),
            pltpu.VMEM((LOWER, *square), F32),
            pltpu.VMEM((PANELS, *square), BF16),
            pltpu.VMEM((COLS, PANELS, *square), BF16),
            pltpu.VMEM((XL * Y, PANELS, *square), BF16),
            pltpu.VMEM((XL * Y, PANELS, *square), BF16),
            pltpu.VMEM((XL * Y, PANELS, *square), F32),
            pltpu.VMEM((XL, Y, PANELS, *square), BF16),
            pltpu.VMEM((Y - 1, XL, PANELS, *square), BF16),
            pltpu.VMEM((XL, PANELS, *square), F32),
            pltpu.VMEM((PANELS, *square), F32),
            pltpu.VMEM((UPPER, *square), BF16),
            pltpu.VMEM((LOWER, *square), F32),
            pltpu.VMEM((LOWER, *square), F32),
            pltpu.VMEM((FIRST_ROWS, BLOCK), F32),
            pltpu.VMEM((SECOND_ROWS, BLOCK), F32),
            pltpu.VMEM((THIRD_ROWS, BLOCK), F32),
            pltpu.SemaphoreType.DMA((7,)),
            pltpu.SemaphoreType.DMA((NC,)),
            pltpu.SemaphoreType.DMA((NC, 2, UP)),
            pltpu.SemaphoreType.DMA((NC,)),
            pltpu.SemaphoreType.DMA((1,)),
            pltpu.SemaphoreType.DMA((NC,)),
            pltpu.SemaphoreType.DMA((1,)),
            pltpu.SemaphoreType.DMA((NC,)),
            pltpu.SemaphoreType.DMA((1,)),
            pltpu.SemaphoreType.DMA((NC,)),
            reduce_scratch(FIRST_ROWS),
            short_reduce_scratch(SECOND_ROWS),
            short_reduce_scratch(THIRD_ROWS),
        ],
        compiler_params=pltpu.CompilerParams(
            collective_id=0, has_side_effects=True, vmem_limit_bytes=62 * 1024 * 1024
        ),
        name="sweep",
    )(
        top_inverse.reshape(COLS, XL * Y, 2, *square),
        upper_panel.reshape(UPPER, *square),
        upper_pattern.reshape(UPPER),
        upper_diagonal,
        lower_panel.reshape(LOWER, *square),
        lower_pattern.reshape(LOWER),
        parents,
        parent_panel,
        lower_diagonal,
    )
    outs = pl.pallas_call(
        finalize,
        out_shape=out_shape,
        in_specs=[vector] * 5,
        out_specs=(vector,) * 5,
        name="finalize",
    )(*outs)
    return (
        outs[0].reshape(UPPER, 1, 1, *square),
        outs[1],
        outs[2].reshape(LOWER, 1, 1, *square),
        outs[3],
        outs[4],
    )


def solution(mesh):
    return jax.shard_map(
        per_device,
        mesh=mesh,
        in_specs=(
            P("row", None, None, "col", None, None),
            P(None, "row", "col", None, None),
            P(None, "row", "col"),
            P(),
            P(None, "row", "col", None, None),
            P(None, "row", "col"),
            P(),
            P(),
            P(),
        ),
        out_specs=(
            P(None, "row", "col", None, None),
            P(),
            P(None, "row", "col", None, None),
            P(),
            P(),
        ),
        check_vma=False,
    )
```

time: 157 us -> 112 us (0.71)
  Pallas kernels: 145 us -> 111 us
  local copies, waits for them, and re-layouts: 11.2 us -> 0 us
    pallas_call x1 -> x2, Pallas kernels: 145 us -> 111 us  [the longest x1 108 us: per_device(): pl.pallas_call(kernel, out_shape=out_shape, in_specs=[anywhere, anywhere,...]
    unnamed x7 -> x0, local copies, waits for them, and re-layouts: 11.2 us -> none
where the time goes in v2:
time: 112 us
  Pallas kernels  111 us (99%)
    pallas_call x1, Pallas kernels, per_device(): pl.pallas_call(kernel, out_shape=out_shape, in_specs=[anywhere, anywhere,...  108 us
    pallas_call x1, Pallas kernels, per_device(): pl.pallas_call(finalize, out_shape=out_shape, in_specs=[vector] * 5, out_...  2.58 us

profile of v2, /device:TPU:1, one launch (start us, length us, event | category | flops | bytes accessed | tf_op | source)
XLA Modules:
  0.0 111.7 jit_solution(140690401090733808)
XLA Ops:
  0.6 108.4 %sweep.1 = (bf16[3,128,128]{2,1,0:T(8,128)(2,1)}, f32[3,128,128]{2,1,0:T(8,128)}, bf16[8,128,128]{2,1,0:T(8,128)(2,1)}, f32[8,128,128]{2,1,0:T(8,128)}, f32[8,128,128]{2,1,0:T(8,128)}) custom-call(bf16[16,8,2,128,128]{4,3,2,1,0:T(8,128)(2,1)} %bitcast.11, bf16[3,128,128]{2,1,0:T(8,128)(2,1)} %bitcast.13, s32[3]{0:T(128)} %bitcast.14, ...), custom_call_target="tpu_custom_call" | custom-call | tf_op jit(solution)/shard_map/sweep/pallas_call | solution.py:599
  109.1 2.6 %finalize.1 = (bf16[3,128,128]{2,1,0:T(8,128)(2,1)}, f32[3,128,128]{2,1,0:T(8,128)}, bf16[8,128,128]{2,1,0:T(8,128)(2,1)}, f32[8,128,128]{2,1,0:T(8,128)}, f32[8,128,128]{2,1,0:T(8,128)}) custom-call(bf16[3,128,128]{2,1,0:T(8,128)(2,1)} %get-tuple-element.15.refs_0_, f32[3,128,128]{2,1,0:T(8,128)} %get-tuple-element.16.refs_1_, ...), custom_call_target="tpu_custom_call" | custom-call | tf_op jit(solution)/shard_map/finalize/pallas_call | solution.py:656

commit v3 on v2

--- a/solution.py
+++ b/solution.py
@@ -20,28 +20,28 @@
 PANELS = UPPER + LOWER
 UP, DOWN = Z // 2, Z // 2 - 1
 
-CHUNKS = ((0, 1), (1, 2), (3, 2), (5, 2), (7, 2), (9, 1), (10, 1))
-SPREAD = (True, False, True, True, False, True, False)
+CHUNKS = ((0, 2), (2, 1), (3, 2), (5, 2), (7, 2), (9, 1), (10, 1))
+SPREAD = (True, True, False, True, False, True, False)
 NC = len(CHUNKS)
-LATE = 4
+LATE = 2
 ORDER = (
     ("seed", 0), ("seed", 1), ("seed", 2), ("ring", 0, 0, 1), ("ring", 1, 0, 1),
-    ("seed_other", 1), ("ring", 2, 0, 1), ("ring", 0, 0, 2), ("ring", 1, 0, 2),
-    ("ring", 1, 1, 1), ("ring", 2, 0, 2), ("ring", 0, 0, 3), ("ring", 1, 0, 3),
-    ("ring", 1, 1, 2), ("ring", 2, 0, 3), ("ring", 0, 0, 4), ("ring", 1, 0, 4), ("seed", 3),
-    ("ring", 1, 1, 3), ("ring", 2, 0, 4), ("seed", 4), ("m0", 0), ("ring", 3, 0, 1), ("m1", 0),
-    ("ring", 1, 1, 4), ("m0", 1), ("ring", 3, 0, 2), ("ring", 4, 0, 1), ("seed_other", 4),
-    ("e", 0), ("m1", 1), ("m0", 2), ("ring", 3, 0, 3), ("e", 1), ("m1", 2), ("ring", 4, 0, 2),
-    ("ring", 4, 1, 1), ("f", 0), ("e", 2), ("ring", 3, 0, 4), ("seed", 5), ("ring", 4, 0, 3),
-    ("h", 0), ("ring", 4, 1, 2), ("ring", 5, 0, 1), ("m0", 3), ("ring", 4, 0, 4), ("seed", 6),
-    ("f", 1), ("ring", 4, 1, 3), ("m1", 3), ("ring", 5, 0, 2), ("ring", 6, 0, 1), ("e", 3),
-    ("seed_other", 6), ("ring", 4, 1, 4), ("m0", 4), ("ring", 5, 0, 3), ("ring", 6, 0, 2),
-    ("h", 1), ("ring", 6, 1, 1), ("cross",), ("f", 2), ("a", 0), ("m1", 4), ("ring", 5, 0, 4),
-    ("ring", 6, 0, 3), ("e", 4), ("ring", 6, 1, 2), ("a", 1), ("ring", 6, 0, 4), ("f", 3),
-    ("h", 2), ("ring", 6, 1, 3), ("m0", 5), ("ring", 6, 1, 4), ("m1", 5), ("m0", 6), ("e", 5),
-    ("m1", 6), ("f", 4), ("e", 6), ("h", 3), ("b", 0), ("h", 4), ("a", 2), ("f", 5), ("f", 6),
-    ("h", 5), ("h", 6), ("c", 0), ("a", 3), ("b", 1), ("b", 2), ("c", 1), ("a", 4), ("c", 2),
-    ("a", 5), ("b", 3), ("c", 3),
+    ("ring", 2, 0, 1), ("seed_other", 2), ("ring", 0, 0, 2), ("ring", 1, 0, 2),
+    ("ring", 2, 0, 2), ("ring", 2, 1, 1), ("ring", 0, 0, 3), ("ring", 1, 0, 3),
+    ("ring", 2, 0, 3), ("ring", 2, 1, 2), ("ring", 0, 0, 4), ("ring", 1, 0, 4), ("seed", 3),
+    ("ring", 2, 0, 4), ("seed", 4), ("ring", 2, 1, 3), ("m0", 0), ("ring", 3, 0, 1), ("m1", 0),
+    ("ring", 2, 1, 4), ("ring", 4, 0, 1), ("seed_other", 4), ("m0", 1), ("m1", 1),
+    ("ring", 3, 0, 2), ("e", 0), ("m0", 2), ("ring", 4, 0, 2), ("ring", 4, 1, 1), ("e", 1),
+    ("m1", 2), ("ring", 3, 0, 3), ("ring", 4, 0, 3), ("e", 2), ("ring", 4, 1, 2),
+    ("ring", 3, 0, 4), ("f", 0), ("ring", 4, 0, 4), ("seed", 5), ("seed", 6), ("ring", 4, 1, 3),
+    ("f", 1), ("m0", 3), ("ring", 5, 0, 1), ("ring", 6, 0, 1), ("m1", 3), ("ring", 4, 1, 4),
+    ("h", 0), ("m0", 4), ("ring", 5, 0, 2), ("ring", 6, 0, 2), ("seed_other", 6), ("h", 1),
+    ("cross",), ("f", 2), ("e", 3), ("a", 0), ("m1", 4), ("ring", 5, 0, 3), ("ring", 6, 0, 3),
+    ("ring", 6, 1, 1), ("e", 4), ("ring", 5, 0, 4), ("ring", 6, 0, 4), ("a", 1), ("h", 2),
+    ("ring", 6, 1, 2), ("ring", 6, 1, 3), ("m0", 5), ("f", 3), ("m1", 5), ("ring", 6, 1, 4),
+    ("m0", 6), ("m1", 6), ("e", 5), ("f", 4), ("h", 3), ("e", 6), ("h", 4), ("b", 0), ("a", 2),
+    ("f", 5), ("f", 6), ("h", 5), ("h", 6), ("c", 0), ("a", 3), ("b", 1), ("c", 1), ("b", 2),
+    ("a", 4), ("c", 2), ("a", 5), ("b", 3), ("c", 3),
 )
 FIRST_ROWS = 1536
 SECOND_ROWS = (LOWER - LATE) * BLOCK

time: 112 us -> 111 us (level)
  no operation moved by 1% of the time
where the time goes in v3:
time: 111 us
  Pallas kernels  110 us (99%)
    pallas_call x1, Pallas kernels, per_device(): pl.pallas_call(kernel, out_shape=out_shape, in_specs=[anywhere, anywhere,...  108 us
    pallas_call x1, Pallas kernels, per_device(): pl.pallas_call(finalize, out_shape=out_shape, in_specs=[vector] * 5, out_...  2.58 us

profile of v3, /device:TPU:1, one launch (start us, length us, event | category | flops | bytes accessed | tf_op | source)
XLA Modules:
  0.0 110.9 jit_solution(17347740906080529057)
XLA Ops:
  0.6 107.7 %sweep.1 = (bf16[3,128,128]{2,1,0:T(8,128)(2,1)}, f32[3,128,128]{2,1,0:T(8,128)}, bf16[8,128,128]{2,1,0:T(8,128)(2,1)}, f32[8,128,128]{2,1,0:T(8,128)}, f32[8,128,128]{2,1,0:T(8,128)}) custom-call(bf16[16,8,2,128,128]{4,3,2,1,0:T(8,128)(2,1)} %bitcast.11, bf16[3,128,128]{2,1,0:T(8,128)(2,1)} %bitcast.13, s32[3]{0:T(128)} %bitcast.14, ...), custom_call_target="tpu_custom_call" | custom-call | tf_op jit(solution)/shard_map/sweep/pallas_call | solution.py:599
  108.4 2.6 %finalize.1 = (bf16[3,128,128]{2,1,0:T(8,128)(2,1)}, f32[3,128,128]{2,1,0:T(8,128)}, bf16[8,128,128]{2,1,0:T(8,128)(2,1)}, f32[8,128,128]{2,1,0:T(8,128)}, f32[8,128,128]{2,1,0:T(8,128)}) custom-call(bf16[3,128,128]{2,1,0:T(8,128)(2,1)} %get-tuple-element.15.refs_0_, f32[3,128,128]{2,1,0:T(8,128)} %get-tuple-element.16.refs_1_, ...), custom_call_target="tpu_custom_call" | custom-call | tf_op jit(solution)/shard_map/finalize/pallas_call | solution.py:656
